TPU v7x, 32 devices: a whole 2x2x4 slice. The times are simulated.
32 devices in a mesh: mesh: 8 (over y, x, core), band: 4 (over z).
Axes of the slice: x: 2, y: 2, z: 4, core: 2. Of those that a mesh axis runs over, the one named last changes fastest.
Arguments:
- states: float32 [2, 64, 8192], P(None, 'band', 'mesh'), may hold values from -6 to 6
- frozen: float32 [2, 32, 8192], P(None, 'band', 'mesh'), may hold values from -0.125 to 0.125
- weights: float32 [8, 8192], P(None, 'mesh'), may hold values from 0.1 to 1
- potential: float32 [8192], P('mesh'), may hold values from -2 to 2
- send_list: int32 [8, 8, 256], P('mesh'), may hold values from 0 to 1023
- neighbours: int32 [8, 8192], P(None, 'mesh'), may hold values from 0 to 3071, as said below
Outputs:
- evolved: float32 [2, 64, 8192], P(None, 'band', 'mesh')
Inputs may be any that keep to these rules, and one draw needn't show every extreme that they name: `neighbours`: an entry below 1024 names a point of the same part; an entry 1024 + s * 256 + c names ghost slot c from part s, where part s is at most 3 parts away in the cyclic order of parts or exactly half the number of parts away, and every part names ghost slots from all those parts. Slots of send_list[s, i] that part i never names hold arbitrary points of part s.
All inputs are finite; a program needn't handle non-finite values.
Results may differ from a plain program's by a relative error of at most 0.0001.
Values sent between devices are 32-bit elements; how exact they have to be, the bound alone decides.
No kernel may reach another device: no remote copies, remote signals or barrier semaphores. Data moves between devices by JAX's collectives and lax.ppermute only.
A program may use at most 128 MiB of HBM per device.

v0:
```python
import jax
import jax.numpy as jnp
from jax import lax
from jax.sharding import PartitionSpec as P

NBRS = 8
TERMS = 4
time_step = 0.3


def rotate(field):
    return jnp.stack([field[1], -field[0]])


def body(states, frozen, weights, potential, send_list, neighbours):
    parts = lax.axis_size("mesh")
    rows = states.shape[1]
    capacity = send_list.shape[2]
    routes = send_list[0]
    full_frozen = lax.all_gather(frozen, "band", axis=1, tiled=True)
    total = states
    term = states
    for order in range(1, TERMS + 1):
        paired = jnp.stack([term, rotate(term)])
        partial_intersection = jnp.einsum(
            "cmp,ocjp->omj", full_frozen, paired, precision=lax.Precision.HIGHEST
        )
        intersection = lax.psum(partial_intersection, "mesh")
        packed = jnp.take(term, routes.reshape(-1), axis=2).reshape(2, rows, parts, capacity)
        arrived = lax.all_to_all(packed, "mesh", split_axis=2, concat_axis=2, tiled=True)
        extended = jnp.concatenate([term, arrived.reshape(2, rows, parts * capacity)], axis=2)
        stencil = jnp.zeros_like(term)
        for apply_order in range(NBRS):
            stencil = stencil + weights[apply_order] * (
                jnp.take(extended, neighbours[apply_order], axis=2) - term
            )
        blocks = jnp.stack(
            [
                jnp.stack([intersection[0], -intersection[1]]),
                jnp.stack([intersection[1], intersection[0]]),
            ]
        )
        exchange = jnp.einsum("dmp,cdmj->cjp", full_frozen, blocks, precision=lax.Precision.HIGHEST)
        image = -0.5 * stencil + potential * term - exchange
        term = time_step / order * rotate(image)
        total = total + term
    return total


def solution(mesh):
    return jax.shard_map(
        body,
        mesh=mesh,
        in_specs=(
            P(None, "band", "mesh"),
            P(None, "band", "mesh"),
            P(None, "mesh"),
            P("mesh"),
            P("mesh", None, None),
            P(None, "mesh"),
        ),
        out_specs=P(None, "band", "mesh"),
        check_vma=False,
    )
```

profile of v0, /device:TPU:0, one launch (start us, length us, event | category | flops | bytes accessed | tf_op | source)
XLA Modules:
  0.0 581.9 jit_solution(13586005560089532101)
XLA Ops:
  2.1 14.4 %gather_fusion = f32[2048,2,16]{2,1,0:T(2,128)} fusion(f32[2,16,1024]{1,0,2:T(2,128)S(1)} %copy.119, s32[2048]{0:T(1024)S(1)} %fusion.108), kind=kCustom, calls=%fused_computation.clone | custom fusion | bytes 532480 | tf_op jit(solution)/shard_map/jit(_take)/gather | solution.py:29
  16.5 10.0 %broadcast_select_fusion.3 = f32[2048,2,16]{2,1,0:T(2,128)S(1)} fusion(f32[2048,2,16]{2,1,0:T(2,128)} %gather_fusion, pred[2048]{0:T(1024)(128)(4,1)S(1)} %compare_and_fusion), kind=kLoop, calls=%fused_computation.39 | loop fusion | flops 65536 | bytes 526336 | tf_op jit(solution)/shard_map/jit(_take)/select_n | solution.py:29
  28.5 5.2 all-to-all-start
  39.6 14.2 %all_gather.3 = f32[2,32,1024]{2,1,0:T(8,128)S(1)} all-gather(f32[2,8,1024]{2,1,0:T(8,128)S(1)} %copy-done.34), channel_id=1, replica_groups=mesh['mesh'=8,'band'=4] {'band'}, dimensions={1}, use_global_device_ids=true | all-gather | bytes 327680 | tf_op jit(solution)/shard_map/all_gather | solution.py:20
  54.3 23.0 %psum.28 = f32[2,32,16]{1,2,0:T(8,128)S(1)} all-reduce(f32[2,32,16]{1,2,0:T(8,128)S(1)} %convolution_bitcast_fusion.7), channel_id=1, replica_groups=mesh['mesh'=8,'band'=4] {'mesh'}, use_global_device_ids=true, to_apply=%region_0.3 | all-reduce | flops 1024 | bytes 8192 | tf_op jit(solution)/shard_map/psum | solution.py:28
  79.9 4.1 copy.122
  84.0 7.6 %gather_fusion.1 = f32[1024,2,16]{2,1,0:T(2,128)} fusion(f32[2,16,3072]{1,0,2:T(2,128)S(1)} %copy.122, s32[1024]{0:T(1024)} %fusion.109), kind=kCustom, calls=%fused_computation.1.clone | custom fusion | bytes 266240 | tf_op jit(solution)/shard_map/jit(_take)/gather | solution.py:35
  93.7 7.6 %gather_fusion.2 = f32[1024,2,16]{2,1,0:T(2,128)} fusion(f32[2,16,3072]{1,0,2:T(2,128)S(1)} %copy.122, s32[1024]{0:T(1024)} %fusion.110), kind=kCustom, calls=%fused_computation.5.clone | custom fusion | bytes 266240 | tf_op jit(solution)/shard_map/jit(_take)/gather | solution.py:35
  103.3 7.6 %gather_fusion.3 = f32[1024,2,16]{2,1,0:T(2,128)} fusion(f32[2,16,3072]{1,0,2:T(2,128)S(1)} %copy.122, s32[1024]{0:T(1024)} %fusion.111), kind=kCustom, calls=%fused_computation.6.clone | custom fusion | bytes 266240 | tf_op jit(solution)/shard_map/jit(_take)/gather | solution.py:35
  110.9 2.0 copy.127
  112.9 7.6 %gather_fusion.4 = f32[1024,2,16]{2,1,0:T(2,128)} fusion(f32[2,16,3072]{1,0,2:T(2,128)S(1)} %copy.122, s32[1024]{0:T(1024)} %fusion.112), kind=kCustom, calls=%fused_computation.7.clone | custom fusion | bytes 266240 | tf_op jit(solution)/shard_map/jit(_take)/gather | solution.py:35
  122.5 7.6 %gather_fusion.5 = f32[1024,2,16]{2,1,0:T(2,128)} fusion(f32[2,16,3072]{1,0,2:T(2,128)S(1)} %copy.122, s32[1024]{0:T(1024)} %fusion.113), kind=kCustom, calls=%fused_computation.8.clone | custom fusion | bytes 266240 | tf_op jit(solution)/shard_map/jit(_take)/gather | solution.py:35
  132.1 7.6 %gather_fusion.6 = f32[1024,2,16]{2,1,0:T(2,128)} fusion(f32[2,16,3072]{1,0,2:T(2,128)S(1)} %copy.122, s32[1024]{0:T(1024)} %fusion.114), kind=kCustom, calls=%fused_computation.9.clone | custom fusion | bytes 266240 | tf_op jit(solution)/shard_map/jit(_take)/gather | solution.py:35
  141.7 7.5 %gather_fusion.7 = f32[1024,2,16]{2,1,0:T(2,128)} fusion(f32[2,16,3072]{1,0,2:T(2,128)S(1)} %copy.122, s32[1024]{0:T(1024)S(1)} %fusion.115), kind=kCustom, calls=%fused_computation.10.clone | custom fusion | bytes 266240 | tf_op jit(solution)/shard_map/jit(_take)/gather | solution.py:35
  151.2 7.5 %gather_fusion.8 = f32[1024,2,16]{2,1,0:T(2,128)} fusion(f32[2,16,3072]{1,0,2:T(2,128)S(1)} %copy.122, s32[1024]{0:T(1024)S(1)} %fusion.116), kind=kCustom, calls=%fused_computation.11.clone | custom fusion | bytes 266240 | tf_op jit(solution)/shard_map/jit(_take)/gather | solution.py:35
  163.5 22.3 %psum.29 = f32[2,32,16]{1,2,0:T(8,128)S(1)} all-reduce(f32[2,32,16]{1,2,0:T(8,128)S(1)} %convolution_bitcast_fusion.6), channel_id=1, replica_groups=mesh['mesh'=8,'band'=4] {'mesh'}, use_global_device_ids=true, to_apply=%region_1.4 | all-reduce | flops 1024 | bytes 8192 | tf_op jit(solution)/shard_map/psum | solution.py:28
  185.8 14.4 %gather_fusion.9 = f32[2048,2,16]{2,1,0:T(2,128)} fusion(f32[2,16,1024]{1,0,2:T(2,128)S(1)} %copy.138, s32[2048]{0:T(1024)S(1)} %fusion.108), kind=kCustom, calls=%fused_computation.2.clone | custom fusion | bytes 532480 | tf_op jit(solution)/shard_map/jit(_take)/gather | solution.py:29
  200.2 10.0 %broadcast_select_fusion.2 = f32[2048,2,16]{2,1,0:T(2,128)S(1)} fusion(f32[2048,2,16]{2,1,0:T(2,128)} %gather_fusion.9, pred[2048]{0:T(1024)(128)(4,1)S(1)} %copy-done.36), kind=kLoop, calls=%fused_computation.38 | loop fusion | flops 65536 | bytes 526336 | tf_op jit(solution)/shard_map/jit(_take)/select_n | solution.py:29
  212.1 3.6 all-to-all-start.1
  216.3 6.1 %all-to-all-done.1 = f32[2,16,8,256]{3,1,0,2:T(8,128)S(1)} async-done(((f32[2,16,8,256]{3,1,0,2:T(8,128)}), f32[2,16,8,256]{3,1,0,2:T(8,128)S(1)}, u32[]{:S(2)}, u32[]{:S(2)}) %all-to-all-start.1) | async-done | bytes 262176 | tf_op jit(solution)/shard_map/all_to_all | solution.py:30
  223.2 4.1 copy.141
  227.3 7.6 %gather_fusion.10 = f32[1024,2,16]{2,1,0:T(2,128)} fusion(f32[2,16,3072]{1,0,2:T(2,128)S(1)} %copy.141, s32[1024]{0:T(1024)} %fusion.109), kind=kCustom, calls=%fused_computation.12.clone | custom fusion | bytes 266240 | tf_op jit(solution)/shard_map/jit(_take)/gather | solution.py:35
  235.0 7.6 %gather_fusion.11 = f32[1024,2,16]{2,1,0:T(2,128)} fusion(f32[2,16,3072]{1,0,2:T(2,128)S(1)} %copy.141, s32[1024]{0:T(1024)} %fusion.110), kind=kCustom, calls=%fused_computation.13.clone | custom fusion | bytes 266240 | tf_op jit(solution)/shard_map/jit(_take)/gather | solution.py:35
  242.6 7.6 %gather_fusion.12 = f32[1024,2,16]{2,1,0:T(2,128)} fusion(f32[2,16,3072]{1,0,2:T(2,128)S(1)} %copy.141, s32[1024]{0:T(1024)} %fusion.111), kind=kCustom, calls=%fused_computation.14.clone | custom fusion | bytes 266240 | tf_op jit(solution)/shard_map/jit(_take)/gather | solution.py:35
  250.2 7.6 %gather_fusion.13 = f32[1024,2,16]{2,1,0:T(2,128)} fusion(f32[2,16,3072]{1,0,2:T(2,128)S(1)} %copy.141, s32[1024]{0:T(1024)} %fusion.112), kind=kCustom, calls=%fused_computation.15.clone | custom fusion | bytes 266240 | tf_op jit(solution)/shard_map/jit(_take)/gather | solution.py:35
  257.8 7.6 %gather_fusion.14 = f32[1024,2,16]{2,1,0:T(2,128)} fusion(f32[2,16,3072]{1,0,2:T(2,128)S(1)} %copy.141, s32[1024]{0:T(1024)} %fusion.113), kind=kCustom, calls=%fused_computation.16.clone | custom fusion | bytes 266240 | tf_op jit(solution)/shard_map/jit(_take)/gather | solution.py:35
  265.4 7.6 %gather_fusion.15 = f32[1024,2,16]{2,1,0:T(2,128)} fusion(f32[2,16,3072]{1,0,2:T(2,128)S(1)} %copy.141, s32[1024]{0:T(1024)} %fusion.114), kind=kCustom, calls=%fused_computation.17.clone | custom fusion | bytes 266240 | tf_op jit(solution)/shard_map/jit(_take)/gather | solution.py:35
  273.0 7.5 %gather_fusion.16 = f32[1024,2,16]{2,1,0:T(2,128)} fusion(f32[2,16,3072]{1,0,2:T(2,128)S(1)} %copy.141, s32[1024]{0:T(1024)S(1)} %fusion.115), kind=kCustom, calls=%fused_computation.18.clone | custom fusion | bytes 266240 | tf_op jit(solution)/shard_map/jit(_take)/gather | solution.py:35
  280.5 7.5 %gather_fusion.17 = f32[1024,2,16]{2,1,0:T(2,128)} fusion(f32[2,16,3072]{1,0,2:T(2,128)S(1)} %copy.141, s32[1024]{0:T(1024)S(1)} %fusion.116), kind=kCustom, calls=%fused_computation.19.clone | custom fusion | bytes 266240 | tf_op jit(solution)/shard_map/jit(_take)/gather | solution.py:35
  288.0 2.1 copy.142
  290.1 2.1 copy.144
  292.2 2.1 copy.146
  303.7 22.3 %psum.30 = f32[2,32,16]{1,2,0:T(8,128)S(1)} all-reduce(f32[2,32,16]{1,2,0:T(8,128)S(1)} %convolution_bitcast_fusion.5), channel_id=1, replica_groups=mesh['mesh'=8,'band'=4] {'mesh'}, use_global_device_ids=true, to_apply=%region_2.5 | all-reduce | flops 1024 | bytes 8192 | tf_op jit(solution)/shard_map/psum | solution.py:28
  326.0 14.4 %gather_fusion.18 = f32[2048,2,16]{2,1,0:T(2,128)} fusion(f32[2,16,1024]{1,0,2:T(2,128)S(1)} %copy.157, s32[2048]{0:T(1024)S(1)} %fusion.108), kind=kCustom, calls=%fused_computation.3.clone | custom fusion | bytes 532480 | tf_op jit(solution)/shard_map/jit(_take)/gather | solution.py:29
  340.4 10.0 %broadcast_select_fusion.1 = f32[2048,2,16]{2,1,0:T(2,128)S(1)} fusion(f32[2048,2,16]{2,1,0:T(2,128)} %gather_fusion.18, pred[2048]{0:T(1024)(128)(4,1)S(1)} %copy-done.37), kind=kLoop, calls=%fused_computation.37 | loop fusion | flops 65536 | bytes 526336 | tf_op jit(solution)/shard_map/jit(_take)/select_n | solution.py:29
  352.3 3.4 all-to-all-start.2
  356.3 6.2 %all-to-all-done.2 = f32[2,16,8,256]{3,1,0,2:T(8,128)S(1)} async-done(((f32[2,16,8,256]{3,1,0,2:T(8,128)}), f32[2,16,8,256]{3,1,0,2:T(8,128)S(1)}, u32[]{:S(2)}, u32[]{:S(2)}) %all-to-all-start.2) | async-done | bytes 262176 | tf_op jit(solution)/shard_map/all_to_all | solution.py:30
  363.4 4.1 copy.160
  367.5 7.6 %gather_fusion.19 = f32[1024,2,16]{2,1,0:T(2,128)} fusion(f32[2,16,3072]{1,0,2:T(2,128)S(1)} %copy.160, s32[1024]{0:T(1024)} %fusion.109), kind=kCustom, calls=%fused_computation.20.clone | custom fusion | bytes 266240 | tf_op jit(solution)/shard_map/jit(_take)/gather | solution.py:35
  375.2 7.6 %gather_fusion.20 = f32[1024,2,16]{2,1,0:T(2,128)} fusion(f32[2,16,3072]{1,0,2:T(2,128)S(1)} %copy.160, s32[1024]{0:T(1024)} %fusion.110), kind=kCustom, calls=%fused_computation.21.clone | custom fusion | bytes 266240 | tf_op jit(solution)/shard_map/jit(_take)/gather | solution.py:35
  382.8 7.6 %gather_fusion.21 = f32[1024,2,16]{2,1,0:T(2,128)} fusion(f32[2,16,3072]{1,0,2:T(2,128)S(1)} %copy.160, s32[1024]{0:T(1024)} %fusion.111), kind=kCustom, calls=%fused_computation.22.clone | custom fusion | bytes 266240 | tf_op jit(solution)/shard_map/jit(_take)/gather | solution.py:35
  390.4 7.6 %gather_fusion.22 = f32[1024,2,16]{2,1,0:T(2,128)} fusion(f32[2,16,3072]{1,0,2:T(2,128)S(1)} %copy.160, s32[1024]{0:T(1024)} %fusion.112), kind=kCustom, calls=%fused_computation.23.clone | custom fusion | bytes 266240 | tf_op jit(solution)/shard_map/jit(_take)/gather | solution.py:35
  398.0 7.6 %gather_fusion.23 = f32[1024,2,16]{2,1,0:T(2,128)} fusion(f32[2,16,3072]{1,0,2:T(2,128)S(1)} %copy.160, s32[1024]{0:T(1024)} %fusion.113), kind=kCustom, calls=%fused_computation.24.clone | custom fusion | bytes 266240 | tf_op jit(solution)/shard_map/jit(_take)/gather | solution.py:35
  405.6 7.6 %gather_fusion.24 = f32[1024,2,16]{2,1,0:T(2,128)} fusion(f32[2,16,3072]{1,0,2:T(2,128)S(1)} %copy.160, s32[1024]{0:T(1024)} %fusion.114), kind=kCustom, calls=%fused_computation.25.clone | custom fusion | bytes 266240 | tf_op jit(solution)/shard_map/jit(_take)/gather | solution.py:35
  413.2 7.5 %gather_fusion.25 = f32[1024,2,16]{2,1,0:T(2,128)} fusion(f32[2,16,3072]{1,0,2:T(2,128)S(1)} %copy.160, s32[1024]{0:T(1024)S(1)} %fusion.115), kind=kCustom, calls=%fused_computation.26.clone | custom fusion | bytes 266240 | tf_op jit(solution)/shard_map/jit(_take)/gather | solution.py:35
  420.7 7.5 %gather_fusion.26 = f32[1024,2,16]{2,1,0:T(2,128)} fusion(f32[2,16,3072]{1,0,2:T(2,128)S(1)} %copy.160, s32[1024]{0:T(1024)S(1)} %fusion.116), kind=kCustom, calls=%fused_computation.27.clone | custom fusion | bytes 266240 | tf_op jit(solution)/shard_map/jit(_take)/gather | solution.py:35
  428.1 2.1 copy.161
  430.2 2.1 copy.163
  432.4 2.1 copy.165
  443.8 22.3 %psum.31 = f32[2,32,16]{1,2,0:T(8,128)S(1)} all-reduce(f32[2,32,16]{1,2,0:T(8,128)S(1)} %convolution_bitcast_fusion.4), channel_id=1, replica_groups=mesh['mesh'=8,'band'=4] {'mesh'}, use_global_device_ids=true, to_apply=%region_3.6 | all-reduce | flops 1024 | bytes 8192 | tf_op jit(solution)/shard_map/psum | solution.py:28
  466.1 14.4 %gather_fusion.27 = f32[2048,2,16]{2,1,0:T(2,128)} fusion(f32[2,16,1024]{1,0,2:T(2,128)S(1)} %copy.176, s32[2048]{0:T(1024)S(1)} %fusion.108), kind=kCustom, calls=%fused_computation.4.clone | custom fusion | bytes 532480 | tf_op jit(solution)/shard_map/jit(_take)/gather | solution.py:29
  480.6 10.0 %broadcast_select_fusion = f32[2048,2,16]{2,1,0:T(2,128)S(1)} fusion(f32[2048,2,16]{2,1,0:T(2,128)} %gather_fusion.27, pred[2048]{0:T(1024)(128)(4,1)S(1)} %copy-done.38), kind=kLoop, calls=%fused_computation.36 | loop fusion | flops 65536 | bytes 526336 | tf_op jit(solution)/shard_map/jit(_take)/select_n | solution.py:29
  492.4 3.8 all-to-all-start.3
  496.8 6.0 %all-to-all-done.3 = f32[2,16,8,256]{3,1,0,2:T(8,128)S(1)} async-done(((f32[2,16,8,256]{3,1,0,2:T(8,128)}), f32[2,16,8,256]{3,1,0,2:T(8,128)S(1)}, u32[]{:S(2)}, u32[]{:S(2)}) %all-to-all-start.3) | async-done | bytes 262176 | tf_op jit(solution)/shard_map/all_to_all | solution.py:30
  503.7 4.1 copy.179
  507.8 7.6 %gather_fusion.28 = f32[1024,2,16]{2,1,0:T(2,128)} fusion(f32[2,16,3072]{1,0,2:T(2,128)S(1)} %copy.179, s32[1024]{0:T(1024)} %fusion.109), kind=kCustom, calls=%fused_computation.28.clone | custom fusion | bytes 266240 | tf_op jit(solution)/shard_map/jit(_take)/gather | solution.py:35
  515.4 7.6 %gather_fusion.29 = f32[1024,2,16]{2,1,0:T(2,128)} fusion(f32[2,16,3072]{1,0,2:T(2,128)S(1)} %copy.179, s32[1024]{0:T(1024)} %fusion.110), kind=kCustom, calls=%fused_computation.29.clone | custom fusion | bytes 266240 | tf_op jit(solution)/shard_map/jit(_take)/gather | solution.py:35
  523.0 7.6 %gather_fusion.30 = f32[1024,2,16]{2,1,0:T(2,128)} fusion(f32[2,16,3072]{1,0,2:T(2,128)S(1)} %copy.179, s32[1024]{0:T(1024)} %fusion.111), kind=kCustom, calls=%fused_computation.30.clone | custom fusion | bytes 266240 | tf_op jit(solution)/shard_map/jit(_take)/gather | solution.py:35
  530.6 7.6 %gather_fusion.31 = f32[1024,2,16]{2,1,0:T(2,128)} fusion(f32[2,16,3072]{1,0,2:T(2,128)S(1)} %copy.179, s32[1024]{0:T(1024)} %fusion.112), kind=kCustom, calls=%fused_computation.31.clone | custom fusion | bytes 266240 | tf_op jit(solution)/shard_map/jit(_take)/gather | solution.py:35
  538.2 7.5 %gather_fusion.32 = f32[1024,2,16]{2,1,0:T(2,128)} fusion(f32[2,16,3072]{1,0,2:T(2,128)S(1)} %copy.179, s32[1024]{0:T(1024)S(1)} %copy-done.29), kind=kCustom, calls=%fused_computation.32.clone | custom fusion | bytes 266240 | tf_op jit(solution)/shard_map/jit(_take)/gather | solution.py:35
  545.7 7.5 %gather_fusion.33 = f32[1024,2,16]{2,1,0:T(2,128)} fusion(f32[2,16,3072]{1,0,2:T(2,128)S(1)} %copy.179, s32[1024]{0:T(1024)S(1)} %copy-done.28), kind=kCustom, calls=%fused_computation.33.clone | custom fusion | bytes 266240 | tf_op jit(solution)/shard_map/jit(_take)/gather | solution.py:35
  553.2 7.5 %gather_fusion.34 = f32[1024,2,16]{2,1,0:T(2,128)} fusion(f32[2,16,3072]{1,0,2:T(2,128)S(1)} %copy.179, s32[1024]{0:T(1024)S(1)} %fusion.115), kind=kCustom, calls=%fused_computation.34.clone | custom fusion | bytes 266240 | tf_op jit(solution)/shard_map/jit(_take)/gather | solution.py:35
  560.7 7.5 %gather_fusion.35 = f32[1024,2,16]{2,1,0:T(2,128)} fusion(f32[2,16,3072]{1,0,2:T(2,128)S(1)} %copy.179, s32[1024]{0:T(1024)S(1)} %fusion.116), kind=kCustom, calls=%fused_computation.35.clone | custom fusion | bytes 266240 | tf_op jit(solution)/shard_map/jit(_take)/gather | solution.py:35
  568.2 2.2 copy.180
  (178 shorter events, 69.4 us)
Async XLA Ops:
  0.7 27.7 %copy-start.35 = (pred[2048]{0:T(1024)(128)(4,1)}, pred[2048]{0:T(1024)(128)(4,1)S(1)}, u32[]{:S(2)}) copy-start(pred[2048]{0:T(1024)(128)(4,1)S(1)} %compare_and_fusion) | copy-start | bytes 6148
  16.5 17.1 %copy-start = (f32[2,16,1024]{2,1,0:T(8,128)S(1)}, f32[2,16,1024]{2,1,0:T(8,128)}, u32[]{:S(2)}) copy-start(f32[2,16,1024]{2,1,0:T(8,128)} %param.10) | copy-start | bytes 393220
  16.5 17.1 %copy-start.39 = (s32[8,1024]{1,0:T(8,128)S(1)}, s32[8,1024]{1,0:T(8,128)}, u32[]{:S(2)}) copy-start(s32[8,1024]{1,0:T(8,128)} %param.15) | copy-start | bytes 98308
  16.5 23.1 %copy-start.34 = (f32[2,8,1024]{2,1,0:T(8,128)S(1)}, f32[2,8,1024]{2,1,0:T(8,128)}, u32[]{:S(2)}) copy-start(f32[2,8,1024]{2,1,0:T(8,128)} %param.11) | copy-start | bytes 196612
  26.5 50.7 %copy-start.41 = (f32[1024]{0:T(1024)S(1)}, f32[1024]{0:T(1024)}, u32[]{:S(2)}) copy-start(f32[1024]{0:T(1024)} %param.13) | copy-start | bytes 12292
  26.6 51.9 %copy-start.40 = (f32[8,1024]{1,0:T(8,128)S(1)}, f32[8,1024]{1,0:T(8,128)}, u32[]{:S(2)}) copy-start(f32[8,1024]{1,0:T(8,128)} %param.12) | copy-start | bytes 98308
  28.5 50.6 %all-to-all-start = ((f32[2,16,8,256]{3,1,0,2:T(8,128)}), f32[2,16,8,256]{3,1,0,2:T(8,128)S(1)}, u32[]{:S(2)}, u32[]{:S(2)}) async-start(f32[2,16,8,256]{3,1,0,2:T(8,128)} %copy.120), calls=%async_computation | async-start | bytes 524288 | tf_op jit(solution)/shard_map/all_to_all | solution.py:30
  158.7 41.6 %copy-start.36 = (pred[2048]{0:T(1024)(128)(4,1)S(1)}, pred[2048]{0:T(1024)(128)(4,1)}, u32[]{:S(2)}) copy-start(pred[2048]{0:T(1024)(128)(4,1)} %copy-done.35) | copy-start | bytes 6148
  161.9 0.6 copy-start.11
  161.9 0.6 copy-start.13
  212.1 10.3 %all-to-all-start.1 = ((f32[2,16,8,256]{3,1,0,2:T(8,128)}), f32[2,16,8,256]{3,1,0,2:T(8,128)S(1)}, u32[]{:S(2)}, u32[]{:S(2)}) async-start(f32[2,16,8,256]{3,1,0,2:T(8,128)} %copy.139), calls=%async_computation.1 | async-start | bytes 524288 | tf_op jit(solution)/shard_map/all_to_all | solution.py:30
  287.9 10.4 %copy-start.9 = (f32[1024,2,16]{2,1,0:T(2,128)S(1)}, f32[1024,2,16]{2,1,0:T(2,128)}, u32[]{:S(2)}) copy-start(f32[1024,2,16]{2,1,0:T(2,128)} %gather_fusion.15) | copy-start | bytes 393220
  290.0 9.3 %copy-start.7 = (f32[1024,2,16]{2,1,0:T(2,128)S(1)}, f32[1024,2,16]{2,1,0:T(2,128)}, u32[]{:S(2)}) copy-start(f32[1024,2,16]{2,1,0:T(2,128)} %gather_fusion.16) | copy-start | bytes 393220
  292.2 7.6 %copy-start.5 = (f32[1024,2,16]{2,1,0:T(2,128)S(1)}, f32[1024,2,16]{2,1,0:T(2,128)}, u32[]{:S(2)}) copy-start(f32[1024,2,16]{2,1,0:T(2,128)} %gather_fusion.17) | copy-start | bytes 393220
  299.8 40.6 %copy-start.37 = (pred[2048]{0:T(1024)(128)(4,1)S(1)}, pred[2048]{0:T(1024)(128)(4,1)}, u32[]{:S(2)}) copy-start(pred[2048]{0:T(1024)(128)(4,1)} %copy-done.35) | copy-start | bytes 6148
  302.1 0.6 copy-start.15
  302.1 0.6 copy-start.17
  352.3 10.3 %all-to-all-start.2 = ((f32[2,16,8,256]{3,1,0,2:T(8,128)}), f32[2,16,8,256]{3,1,0,2:T(8,128)S(1)}, u32[]{:S(2)}, u32[]{:S(2)}) async-start(f32[2,16,8,256]{3,1,0,2:T(8,128)} %copy.158), calls=%async_computation.2 | async-start | bytes 524288 | tf_op jit(solution)/shard_map/all_to_all | solution.py:30
  428.1 10.4 %copy-start.10 = (f32[1024,2,16]{2,1,0:T(2,128)S(1)}, f32[1024,2,16]{2,1,0:T(2,128)}, u32[]{:S(2)}) copy-start(f32[1024,2,16]{2,1,0:T(2,128)} %gather_fusion.24) | copy-start | bytes 393220
  430.2 9.3 %copy-start.8 = (f32[1024,2,16]{2,1,0:T(2,128)S(1)}, f32[1024,2,16]{2,1,0:T(2,128)}, u32[]{:S(2)}) copy-start(f32[1024,2,16]{2,1,0:T(2,128)} %gather_fusion.25) | copy-start | bytes 393220
  432.4 7.6 %copy-start.6 = (f32[1024,2,16]{2,1,0:T(2,128)S(1)}, f32[1024,2,16]{2,1,0:T(2,128)}, u32[]{:S(2)}) copy-start(f32[1024,2,16]{2,1,0:T(2,128)} %gather_fusion.26) | copy-start | bytes 393220
  440.0 40.6 %copy-start.38 = (pred[2048]{0:T(1024)(128)(4,1)S(1)}, pred[2048]{0:T(1024)(128)(4,1)}, u32[]{:S(2)}) copy-start(pred[2048]{0:T(1024)(128)(4,1)} %copy-done.35) | copy-start | bytes 6148
  442.2 0.6 copy-start.19
  442.2 0.6 copy-start.21
  492.4 45.7 %copy-start.29 = (s32[1024]{0:T(1024)S(1)}, s32[1024]{0:T(1024)}, u32[]{:S(2)}) copy-start(s32[1024]{0:T(1024)} %fusion.113) | copy-start | bytes 12292
  492.4 10.4 %all-to-all-start.3 = ((f32[2,16,8,256]{3,1,0,2:T(8,128)}), f32[2,16,8,256]{3,1,0,2:T(8,128)S(1)}, u32[]{:S(2)}, u32[]{:S(2)}) async-start(f32[2,16,8,256]{3,1,0,2:T(8,128)} %copy.177), calls=%async_computation.3 | async-start | bytes 524288 | tf_op jit(solution)/shard_map/all_to_all | solution.py:30
  496.2 49.5 %copy-start.28 = (s32[1024]{0:T(1024)S(1)}, s32[1024]{0:T(1024)}, u32[]{:S(2)}) copy-start(s32[1024]{0:T(1024)} %fusion.114) | copy-start | bytes 12292
  568.2 6.2 %copy-start.1 = (f32[1024,2,16]{2,1,0:T(2,128)S(1)}, f32[1024,2,16]{2,1,0:T(2,128)}, u32[]{:S(2)}) copy-start(f32[1024,2,16]{2,1,0:T(2,128)} %gather_fusion.31) | copy-start | bytes 393220
  568.2 7.3 %copy-start.2 = (f32[1024,2,16]{2,1,0:T(2,128)S(1)}, f32[1024,2,16]{2,1,0:T(2,128)}, u32[]{:S(2)}) copy-start(f32[1024,2,16]{2,1,0:T(2,128)} %gather_fusion.32) | copy-start | bytes 393220
  568.2 8.4 %copy-start.3 = (f32[1024,2,16]{2,1,0:T(2,128)S(1)}, f32[1024,2,16]{2,1,0:T(2,128)}, u32[]{:S(2)}) copy-start(f32[1024,2,16]{2,1,0:T(2,128)} %gather_fusion.33) | copy-start | bytes 393220
  574.4 5.2 copy-start.30
  574.4 5.2 copy-start.31
  574.4 5.2 copy-start.32
  574.4 5.2 copy-start.33
  575.5 3.6 copy-start.4
  576.6 3.0 copy-start.20
  576.6 3.0 copy-start.22
  576.6 3.0 copy-start.23
  576.6 3.0 copy-start.24
  576.6 3.0 copy-start.25
  576.6 3.0 copy-start.26
  576.6 3.0 copy-start.27
  576.6 4.5 copy-start.12
  576.7 4.5 copy-start.14
  576.7 4.5 copy-start.16
  576.7 4.5 copy-start.18
where the time goes:
time: 585 us; the launch traced here: 582 us
  local copies, waits for them, and re-layouts  382 us (65%)
  blocking collectives  104 us (18%)
  other arithmetic  53 us (9%)
  waiting for transfers between devices  18.3 us (3%)
  starting transfers between devices  15.9 us (3%)
  matrix products  8.07 us (1%)
    gather x64, local copies, waits for them, and re-layouts, body(): jnp.take(extended, neighbours[apply_order], axis=2) - term  293 us
    psum x4, blocking collectives, body(): intersection = lax.psum(partial_intersection, 'mesh')  89.9 us
    gather x4, local copies, waits for them, and re-layouts, body(): jnp.take(term, routes.reshape(-1), axis=2).reshape(2, rows, parts, capacity)  57.7 us
    select_n x4, other arithmetic, body(): jnp.take(term, routes.reshape(-1), axis=2).reshape(2, rows, parts, capacity)  39.9 us
    all_to_all x4, waiting for transfers between devices, body(): lax.all_to_all(packed, 'mesh', split_axis=2, concat_axis=2, tiled=True)  18.3 us
    concatenate x4, local copies, waits for them, and re-layouts, body(): jnp.concatenate([term, arrived.reshape(2, rows, parts * capacity)], axis=2)  16.6 us
    all_to_all x4, starting transfers between devices, body(): lax.all_to_all(packed, 'mesh', split_axis=2, concat_axis=2, tiled=True)  15.9 us
    all_gather x1, blocking collectives, body(): full_frozen = lax.all_gather(frozen, 'band', axis=1, tiled=True)  14.2 us
  transfers between devices with their start and end apart: 4, of which 3 were waited for; matrix products, arithmetic and copies ran while one was open for 2% of the time, Pallas kernels for 0%

commit v1 on v0

--- a/solution.py
+++ b/solution.py
@@ -1,3 +1,4 @@
+import functools
 import jax
 import jax.numpy as jnp
 from jax import lax
@@ -6,6 +7,24 @@
 NBRS = 8
 TERMS = 4
 time_step = 0.3
+
+
+def finish_face(block_in, axis_id):
+    degree = lax.axis_size(axis_id)
+
+    def get_sheets(mid_arr, r2):
+        if r2 >= degree:
+            return mid_arr
+        return get_sheets(
+            mid_arr
+            + lax.ppermute(mid_arr, axis_id, tuple(((dev, dev ^ r2) for dev in range(degree)))),
+            2 * r2,
+        )
+
+    return get_sheets(block_in, 1)
+
+
+set_task_over_axis = functools.partial(finish_face, axis_id="mesh")
 
 
 def rotate(field):
@@ -25,7 +44,7 @@
         partial_intersection = jnp.einsum(
             "cmp,ocjp->omj", full_frozen, paired, precision=lax.Precision.HIGHEST
         )
-        intersection = lax.psum(partial_intersection, "mesh")
+        intersection = set_task_over_axis(partial_intersection)
         packed = jnp.take(term, routes.reshape(-1), axis=2).reshape(2, rows, parts, capacity)
         arrived = lax.all_to_all(packed, "mesh", split_axis=2, concat_axis=2, tiled=True)
         extended = jnp.concatenate([term, arrived.reshape(2, rows, parts * capacity)], axis=2)

time: 585 us -> 515 us (0.88)
  blocking collectives: 104 us -> 15.8 us
  starting transfers between devices: 15.9 us -> 25.2 us
  waiting for transfers between devices: 18.3 us -> 24.4 us
    psum x4 -> x0, blocking collectives: 89.9 us -> none  [body(): intersection = lax.psum(partial_intersection, 'mesh')]
    ppermute x0 -> x12, starting transfers between devices: none -> 10.4 us  [get_sheets(): lax.ppermute(mid_arr, axis_id, tuple(((dev, dev ^ r2) for dev in range(de...]
  transfers between devices with their start and end apart: 4 -> 16, of which waited for: 3 -> 8; matrix products, arithmetic and copies ran while one was open for 2% -> 23% of each run, Pallas kernels for 0% -> 0%
where the time goes in v1:
time: 515 us; the launch traced here: 512 us
  local copies, waits for them, and re-layouts  381 us (74%)
  other arithmetic  55.1 us (11%)
  starting transfers between devices  25.2 us (5%)
  waiting for transfers between devices  24.4 us (5%)
  blocking collectives  15.8 us (3%)
  matrix products  9.01 us (2%)
    gather x64, local copies, waits for them, and re-layouts, body(): jnp.take(extended, neighbours[apply_order], axis=2) - term  295 us
    gather x4, local copies, waits for them, and re-layouts, body(): jnp.take(term, routes.reshape(-1), axis=2).reshape(2, rows, parts, capacity)  58 us
    select_n x4, other arithmetic, body(): jnp.take(term, routes.reshape(-1), axis=2).reshape(2, rows, parts, capacity)  39.9 us
    all_to_all x4, waiting for transfers between devices, body(): lax.all_to_all(packed, 'mesh', split_axis=2, concat_axis=2, tiled=True)  18.6 us
    concatenate x4, local copies, waits for them, and re-layouts, body(): jnp.concatenate([term, arrived.reshape(2, rows, parts * capacity)], axis=2)  16.6 us
    all_gather x1, blocking collectives, body(): full_frozen = lax.all_gather(frozen, 'band', axis=1, tiled=True)  15.8 us
    all_to_all x4, starting transfers between devices, body(): lax.all_to_all(packed, 'mesh', split_axis=2, concat_axis=2, tiled=True)  14.8 us
    ppermute x12, starting transfers between devices, get_sheets(): lax.ppermute(mid_arr, axis_id, tuple(((dev, dev ^ r2) for dev in range(de...  10.4 us
  transfers between devices with their start and end apart: 16, of which 8 were waited for; matrix products, arithmetic and copies ran while one was open for 23% of the time, Pallas kernels for 0%

profile of v1, /device:TPU:0, one launch (start us, length us, event | category | flops | bytes accessed | tf_op | source)
XLA Modules:
  0.0 511.8 jit_solution(14386396467311728361)
XLA Ops:
  0.0 15.8 %all_gather.3 = f32[2,32,1024]{2,1,0:T(8,128)S(1)} all-gather(f32[2,8,1024]{2,1,0:T(8,128)} %param.11), channel_id=1, replica_groups=mesh['mesh'=8,'band'=4] {'band'}, dimensions={1}, use_global_device_ids=true | all-gather | bytes 327680 | tf_op jit(solution)/shard_map/all_gather | solution.py:39
  20.2 14.5 %gather_fusion = f32[2048,2,16]{2,1,0:T(2,128)} fusion(f32[2,16,1024]{1,0,2:T(2,128)S(1)} %copy.119, s32[2048]{0:T(1024)S(1)} %fusion.108), kind=kCustom, calls=%fused_computation.clone | custom fusion | bytes 532480 | tf_op jit(solution)/shard_map/jit(_take)/gather | solution.py:48
  34.7 10.0 %broadcast_select_fusion.3 = f32[2048,2,16]{2,1,0:T(2,128)S(1)} fusion(f32[2048,2,16]{2,1,0:T(2,128)} %gather_fusion, pred[2048]{0:T(1024)(128)(4,1)S(1)} %compare_and_fusion), kind=kLoop, calls=%fused_computation.39 | loop fusion | flops 65536 | bytes 526336 | tf_op jit(solution)/shard_map/jit(_take)/select_n | solution.py:48
  46.6 3.8 all-to-all-start
  56.9 2.1 collective-permute-start.1
  65.9 4.1 copy.122
  70.0 7.6 %gather_fusion.1 = f32[1024,2,16]{2,1,0:T(2,128)} fusion(f32[2,16,3072]{1,0,2:T(2,128)S(1)} %copy.122, s32[1024]{0:T(1024)} %fusion.109), kind=kCustom, calls=%fused_computation.1.clone | custom fusion | bytes 266240 | tf_op jit(solution)/shard_map/jit(_take)/gather | solution.py:54
  77.6 2.0 copy.123
  79.7 7.6 %gather_fusion.2 = f32[1024,2,16]{2,1,0:T(2,128)} fusion(f32[2,16,3072]{1,0,2:T(2,128)S(1)} %copy.122, s32[1024]{0:T(1024)} %fusion.110), kind=kCustom, calls=%fused_computation.5.clone | custom fusion | bytes 266240 | tf_op jit(solution)/shard_map/jit(_take)/gather | solution.py:54
  89.3 7.6 %gather_fusion.3 = f32[1024,2,16]{2,1,0:T(2,128)} fusion(f32[2,16,3072]{1,0,2:T(2,128)S(1)} %copy.122, s32[1024]{0:T(1024)} %fusion.111), kind=kCustom, calls=%fused_computation.6.clone | custom fusion | bytes 266240 | tf_op jit(solution)/shard_map/jit(_take)/gather | solution.py:54
  98.9 7.6 %gather_fusion.4 = f32[1024,2,16]{2,1,0:T(2,128)} fusion(f32[2,16,3072]{1,0,2:T(2,128)S(1)} %copy.122, s32[1024]{0:T(1024)} %fusion.112), kind=kCustom, calls=%fused_computation.7.clone | custom fusion | bytes 266240 | tf_op jit(solution)/shard_map/jit(_take)/gather | solution.py:54
  108.6 7.6 %gather_fusion.5 = f32[1024,2,16]{2,1,0:T(2,128)} fusion(f32[2,16,3072]{1,0,2:T(2,128)S(1)} %copy.122, s32[1024]{0:T(1024)} %fusion.113), kind=kCustom, calls=%fused_computation.8.clone | custom fusion | bytes 266240 | tf_op jit(solution)/shard_map/jit(_take)/gather | solution.py:54
  116.2 2.0 copy.131
  118.2 7.6 %gather_fusion.6 = f32[1024,2,16]{2,1,0:T(2,128)} fusion(f32[2,16,3072]{1,0,2:T(2,128)S(1)} %copy.122, s32[1024]{0:T(1024)} %fusion.114), kind=kCustom, calls=%fused_computation.9.clone | custom fusion | bytes 266240 | tf_op jit(solution)/shard_map/jit(_take)/gather | solution.py:54
  127.9 7.6 %gather_fusion.7 = f32[1024,2,16]{2,1,0:T(2,128)} fusion(f32[2,16,3072]{1,0,2:T(2,128)S(1)} %copy.122, s32[1024]{0:T(1024)} %fusion.115), kind=kCustom, calls=%fused_computation.10.clone | custom fusion | bytes 266240 | tf_op jit(solution)/shard_map/jit(_take)/gather | solution.py:54
  137.5 7.6 %gather_fusion.8 = f32[1024,2,16]{2,1,0:T(2,128)} fusion(f32[2,16,3072]{1,0,2:T(2,128)S(1)} %copy.122, s32[1024]{0:T(1024)} %fusion.116), kind=kCustom, calls=%fused_computation.11.clone | custom fusion | bytes 266240 | tf_op jit(solution)/shard_map/jit(_take)/gather | solution.py:54
  153.2 14.5 %gather_fusion.9 = f32[2048,2,16]{2,1,0:T(2,128)} fusion(f32[2,16,1024]{1,0,2:T(2,128)S(1)} %copy.138, s32[2048]{0:T(1024)S(1)} %fusion.108), kind=kCustom, calls=%fused_computation.2.clone | custom fusion | bytes 532480 | tf_op jit(solution)/shard_map/jit(_take)/gather | solution.py:48
  169.3 10.0 %broadcast_select_fusion.2 = f32[2048,2,16]{2,1,0:T(2,128)S(1)} fusion(f32[2048,2,16]{2,1,0:T(2,128)} %gather_fusion.9, pred[2048]{0:T(1024)(128)(4,1)S(1)} %copy-done.33), kind=kLoop, calls=%fused_computation.38 | loop fusion | flops 65536 | bytes 526336 | tf_op jit(solution)/shard_map/jit(_take)/select_n | solution.py:48
  181.1 3.6 all-to-all-start.1
  185.4 6.0 %all-to-all-done.1 = f32[2,16,8,256]{3,1,0,2:T(8,128)S(1)} async-done(((f32[2,16,8,256]{3,1,0,2:T(8,128)}), f32[2,16,8,256]{3,1,0,2:T(8,128)S(1)}, u32[]{:S(2)}, u32[]{:S(2)}) %all-to-all-start.1) | async-done | bytes 262176 | tf_op jit(solution)/shard_map/all_to_all | solution.py:49
  192.2 4.1 copy.141
  196.4 7.6 %gather_fusion.10 = f32[1024,2,16]{2,1,0:T(2,128)} fusion(f32[2,16,3072]{1,0,2:T(2,128)S(1)} %copy.141, s32[1024]{0:T(1024)} %fusion.109), kind=kCustom, calls=%fused_computation.12.clone | custom fusion | bytes 266240 | tf_op jit(solution)/shard_map/jit(_take)/gather | solution.py:54
  204.0 7.6 %gather_fusion.11 = f32[1024,2,16]{2,1,0:T(2,128)} fusion(f32[2,16,3072]{1,0,2:T(2,128)S(1)} %copy.141, s32[1024]{0:T(1024)} %fusion.110), kind=kCustom, calls=%fused_computation.13.clone | custom fusion | bytes 266240 | tf_op jit(solution)/shard_map/jit(_take)/gather | solution.py:54
  211.6 7.6 %gather_fusion.12 = f32[1024,2,16]{2,1,0:T(2,128)} fusion(f32[2,16,3072]{1,0,2:T(2,128)S(1)} %copy.141, s32[1024]{0:T(1024)} %fusion.111), kind=kCustom, calls=%fused_computation.14.clone | custom fusion | bytes 266240 | tf_op jit(solution)/shard_map/jit(_take)/gather | solution.py:54
  219.2 7.7 %gather_fusion.13 = f32[1024,2,16]{2,1,0:T(2,128)} fusion(f32[2,16,3072]{1,0,2:T(2,128)S(1)} %copy.141, s32[1024]{0:T(1024)} %fusion.112), kind=kCustom, calls=%fused_computation.15.clone | custom fusion | bytes 266240 | tf_op jit(solution)/shard_map/jit(_take)/gather | solution.py:54
  226.9 7.6 %gather_fusion.14 = f32[1024,2,16]{2,1,0:T(2,128)} fusion(f32[2,16,3072]{1,0,2:T(2,128)S(1)} %copy.141, s32[1024]{0:T(1024)} %fusion.113), kind=kCustom, calls=%fused_computation.16.clone | custom fusion | bytes 266240 | tf_op jit(solution)/shard_map/jit(_take)/gather | solution.py:54
  234.5 7.6 %gather_fusion.15 = f32[1024,2,16]{2,1,0:T(2,128)} fusion(f32[2,16,3072]{1,0,2:T(2,128)S(1)} %copy.141, s32[1024]{0:T(1024)} %fusion.114), kind=kCustom, calls=%fused_computation.17.clone | custom fusion | bytes 266240 | tf_op jit(solution)/shard_map/jit(_take)/gather | solution.py:54
  242.1 7.6 %gather_fusion.16 = f32[1024,2,16]{2,1,0:T(2,128)} fusion(f32[2,16,3072]{1,0,2:T(2,128)S(1)} %copy.141, s32[1024]{0:T(1024)} %fusion.115), kind=kCustom, calls=%fused_computation.18.clone | custom fusion | bytes 266240 | tf_op jit(solution)/shard_map/jit(_take)/gather | solution.py:54
  249.7 7.6 %gather_fusion.17 = f32[1024,2,16]{2,1,0:T(2,128)} fusion(f32[2,16,3072]{1,0,2:T(2,128)S(1)} %copy.141, s32[1024]{0:T(1024)} %fusion.116), kind=kCustom, calls=%fused_computation.19.clone | custom fusion | bytes 266240 | tf_op jit(solution)/shard_map/jit(_take)/gather | solution.py:54
  257.3 2.1 copy.142
  259.4 2.1 copy.144
  261.5 2.1 copy.146
  265.7 2.0 copy.150
  274.3 14.5 %gather_fusion.18 = f32[2048,2,16]{2,1,0:T(2,128)} fusion(f32[2,16,1024]{1,0,2:T(2,128)S(1)} %copy.157, s32[2048]{0:T(1024)S(1)} %fusion.108), kind=kCustom, calls=%fused_computation.3.clone | custom fusion | bytes 532480 | tf_op jit(solution)/shard_map/jit(_take)/gather | solution.py:48
  289.4 10.0 %broadcast_select_fusion.1 = f32[2048,2,16]{2,1,0:T(2,128)S(1)} fusion(f32[2048,2,16]{2,1,0:T(2,128)} %gather_fusion.18, pred[2048]{0:T(1024)(128)(4,1)S(1)} %copy-done.34), kind=kLoop, calls=%fused_computation.37 | loop fusion | flops 65536 | bytes 526336 | tf_op jit(solution)/shard_map/jit(_take)/select_n | solution.py:48
  301.3 3.6 all-to-all-start.2
  305.6 6.3 %all-to-all-done.2 = f32[2,16,8,256]{3,1,0,2:T(8,128)S(1)} async-done(((f32[2,16,8,256]{3,1,0,2:T(8,128)}), f32[2,16,8,256]{3,1,0,2:T(8,128)S(1)}, u32[]{:S(2)}, u32[]{:S(2)}) %all-to-all-start.2) | async-done | bytes 262176 | tf_op jit(solution)/shard_map/all_to_all | solution.py:49
  312.7 4.1 copy.160
  316.8 7.6 %gather_fusion.19 = f32[1024,2,16]{2,1,0:T(2,128)} fusion(f32[2,16,3072]{1,0,2:T(2,128)S(1)} %copy.160, s32[1024]{0:T(1024)} %fusion.109), kind=kCustom, calls=%fused_computation.20.clone | custom fusion | bytes 266240 | tf_op jit(solution)/shard_map/jit(_take)/gather | solution.py:54
  324.4 7.6 %gather_fusion.20 = f32[1024,2,16]{2,1,0:T(2,128)} fusion(f32[2,16,3072]{1,0,2:T(2,128)S(1)} %copy.160, s32[1024]{0:T(1024)} %fusion.110), kind=kCustom, calls=%fused_computation.21.clone | custom fusion | bytes 266240 | tf_op jit(solution)/shard_map/jit(_take)/gather | solution.py:54
  332.1 7.6 %gather_fusion.21 = f32[1024,2,16]{2,1,0:T(2,128)} fusion(f32[2,16,3072]{1,0,2:T(2,128)S(1)} %copy.160, s32[1024]{0:T(1024)} %fusion.111), kind=kCustom, calls=%fused_computation.22.clone | custom fusion | bytes 266240 | tf_op jit(solution)/shard_map/jit(_take)/gather | solution.py:54
  339.7 7.7 %gather_fusion.22 = f32[1024,2,16]{2,1,0:T(2,128)} fusion(f32[2,16,3072]{1,0,2:T(2,128)S(1)} %copy.160, s32[1024]{0:T(1024)} %fusion.112), kind=kCustom, calls=%fused_computation.23.clone | custom fusion | bytes 266240 | tf_op jit(solution)/shard_map/jit(_take)/gather | solution.py:54
  347.3 7.6 %gather_fusion.23 = f32[1024,2,16]{2,1,0:T(2,128)} fusion(f32[2,16,3072]{1,0,2:T(2,128)S(1)} %copy.160, s32[1024]{0:T(1024)} %fusion.113), kind=kCustom, calls=%fused_computation.24.clone | custom fusion | bytes 266240 | tf_op jit(solution)/shard_map/jit(_take)/gather | solution.py:54
  354.9 7.6 %gather_fusion.24 = f32[1024,2,16]{2,1,0:T(2,128)} fusion(f32[2,16,3072]{1,0,2:T(2,128)S(1)} %copy.160, s32[1024]{0:T(1024)} %fusion.114), kind=kCustom, calls=%fused_computation.25.clone | custom fusion | bytes 266240 | tf_op jit(solution)/shard_map/jit(_take)/gather | solution.py:54
  362.5 7.6 %gather_fusion.25 = f32[1024,2,16]{2,1,0:T(2,128)} fusion(f32[2,16,3072]{1,0,2:T(2,128)S(1)} %copy.160, s32[1024]{0:T(1024)} %fusion.115), kind=kCustom, calls=%fused_computation.26.clone | custom fusion | bytes 266240 | tf_op jit(solution)/shard_map/jit(_take)/gather | solution.py:54
  370.1 7.6 %gather_fusion.26 = f32[1024,2,16]{2,1,0:T(2,128)} fusion(f32[2,16,3072]{1,0,2:T(2,128)S(1)} %copy.160, s32[1024]{0:T(1024)} %fusion.116), kind=kCustom, calls=%fused_computation.27.clone | custom fusion | bytes 266240 | tf_op jit(solution)/shard_map/jit(_take)/gather | solution.py:54
  377.8 2.1 copy.161
  379.9 2.1 copy.163
  382.0 2.1 copy.165
  386.1 2.0 copy.169
  394.8 14.5 %gather_fusion.27 = f32[2048,2,16]{2,1,0:T(2,128)} fusion(f32[2,16,1024]{1,0,2:T(2,128)S(1)} %copy.176, s32[2048]{0:T(1024)S(1)} %fusion.108), kind=kCustom, calls=%fused_computation.4.clone | custom fusion | bytes 532480 | tf_op jit(solution)/shard_map/jit(_take)/gather | solution.py:48
  409.9 10.0 %broadcast_select_fusion = f32[2048,2,16]{2,1,0:T(2,128)S(1)} fusion(f32[2048,2,16]{2,1,0:T(2,128)} %gather_fusion.27, pred[2048]{0:T(1024)(128)(4,1)S(1)} %copy-done.35), kind=kLoop, calls=%fused_computation.36 | loop fusion | flops 65536 | bytes 526336 | tf_op jit(solution)/shard_map/jit(_take)/select_n | solution.py:48
  421.8 3.8 all-to-all-start.3
  426.2 6.3 %all-to-all-done.3 = f32[2,16,8,256]{3,1,0,2:T(8,128)S(1)} async-done(((f32[2,16,8,256]{3,1,0,2:T(8,128)}), f32[2,16,8,256]{3,1,0,2:T(8,128)S(1)}, u32[]{:S(2)}, u32[]{:S(2)}) %all-to-all-start.3) | async-done | bytes 262176 | tf_op jit(solution)/shard_map/all_to_all | solution.py:49
  433.3 4.1 copy.179
  437.4 7.6 %gather_fusion.28 = f32[1024,2,16]{2,1,0:T(2,128)} fusion(f32[2,16,3072]{1,0,2:T(2,128)S(1)} %copy.179, s32[1024]{0:T(1024)} %fusion.109), kind=kCustom, calls=%fused_computation.28.clone | custom fusion | bytes 266240 | tf_op jit(solution)/shard_map/jit(_take)/gather | solution.py:54
  445.1 7.6 %gather_fusion.29 = f32[1024,2,16]{2,1,0:T(2,128)} fusion(f32[2,16,3072]{1,0,2:T(2,128)S(1)} %copy.179, s32[1024]{0:T(1024)} %fusion.110), kind=kCustom, calls=%fused_computation.29.clone | custom fusion | bytes 266240 | tf_op jit(solution)/shard_map/jit(_take)/gather | solution.py:54
  452.7 7.5 %gather_fusion.30 = f32[1024,2,16]{2,1,0:T(2,128)} fusion(f32[2,16,3072]{1,0,2:T(2,128)S(1)} %copy.179, s32[1024]{0:T(1024)S(1)} %copy-done.31), kind=kCustom, calls=%fused_computation.30.clone | custom fusion | bytes 266240 | tf_op jit(solution)/shard_map/jit(_take)/gather | solution.py:54
  460.2 7.5 %gather_fusion.31 = f32[1024,2,16]{2,1,0:T(2,128)} fusion(f32[2,16,3072]{1,0,2:T(2,128)S(1)} %copy.179, s32[1024]{0:T(1024)S(1)} %copy-done.30), kind=kCustom, calls=%fused_computation.31.clone | custom fusion | bytes 266240 | tf_op jit(solution)/shard_map/jit(_take)/gather | solution.py:54
  467.7 7.6 %gather_fusion.32 = f32[1024,2,16]{2,1,0:T(2,128)} fusion(f32[2,16,3072]{1,0,2:T(2,128)S(1)} %copy.179, s32[1024]{0:T(1024)} %fusion.113), kind=kCustom, calls=%fused_computation.32.clone | custom fusion | bytes 266240 | tf_op jit(solution)/shard_map/jit(_take)/gather | solution.py:54
  475.3 7.6 %gather_fusion.33 = f32[1024,2,16]{2,1,0:T(2,128)} fusion(f32[2,16,3072]{1,0,2:T(2,128)S(1)} %copy.179, s32[1024]{0:T(1024)} %fusion.114), kind=kCustom, calls=%fused_computation.33.clone | custom fusion | bytes 266240 | tf_op jit(solution)/shard_map/jit(_take)/gather | solution.py:54
  482.9 7.6 %gather_fusion.34 = f32[1024,2,16]{2,1,0:T(2,128)} fusion(f32[2,16,3072]{1,0,2:T(2,128)S(1)} %copy.179, s32[1024]{0:T(1024)} %fusion.115), kind=kCustom, calls=%fused_computation.34.clone | custom fusion | bytes 266240 | tf_op jit(solution)/shard_map/jit(_take)/gather | solution.py:54
  490.5 7.6 %gather_fusion.35 = f32[1024,2,16]{2,1,0:T(2,128)} fusion(f32[2,16,3072]{1,0,2:T(2,128)S(1)} %copy.179, s32[1024]{0:T(1024)} %fusion.116), kind=kCustom, calls=%fused_computation.35.clone | custom fusion | bytes 266240 | tf_op jit(solution)/shard_map/jit(_take)/gather | solution.py:54
  498.1 2.2 copy.180
  (204 shorter events, 78.6 us)
Async XLA Ops:
  18.0 38.9 %collective-permute-start = (f32[2,32,16]{1,2,0:T(8,128)S(1)}, f32[2,32,16]{1,2,0:T(8,128)S(1)}, u32[]{:S(2)}, u32[]{:S(2)}) collective-permute-start(f32[2,32,16]{1,2,0:T(8,128)S(1)} %convolution_bitcast_fusion.7), channel_id=1, source_target_pairs={{0,4},{4,0},{8,12},{12,8},{16,20},{20,16},{24,28},{28,24},{1,5},{5... | collective-permute-start | bytes 12296 | tf_op jit(solution)/shard_map/ppermute | solution.py:20
  20.2 26.4 %copy-start.32 = (pred[2048]{0:T(1024)(128)(4,1)}, pred[2048]{0:T(1024)(128)(4,1)S(1)}, u32[]{:S(2)}) copy-start(pred[2048]{0:T(1024)(128)(4,1)S(1)} %compare_and_fusion) | copy-start | bytes 6148
  34.7 15.7 %copy-start.36 = (s32[8,1024]{1,0:T(8,128)S(1)}, s32[8,1024]{1,0:T(8,128)}, u32[]{:S(2)}) copy-start(s32[8,1024]{1,0:T(8,128)} %param.15) | copy-start | bytes 98308
  34.7 20.4 %copy-start.37 = (f32[8,1024]{1,0:T(8,128)S(1)}, f32[8,1024]{1,0:T(8,128)}, u32[]{:S(2)}) copy-start(f32[8,1024]{1,0:T(8,128)} %param.12) | copy-start | bytes 98308
  34.7 30.4 %copy-start = (f32[2,16,1024]{2,1,0:T(8,128)S(1)}, f32[2,16,1024]{2,1,0:T(8,128)}, u32[]{:S(2)}) copy-start(f32[2,16,1024]{2,1,0:T(8,128)} %param.10) | copy-start | bytes 393220
  46.6 18.5 %all-to-all-start = ((f32[2,16,8,256]{3,1,0,2:T(8,128)}), f32[2,16,8,256]{3,1,0,2:T(8,128)S(1)}, u32[]{:S(2)}, u32[]{:S(2)}) async-start(f32[2,16,8,256]{3,1,0,2:T(8,128)} %copy.120), calls=%async_computation | async-start | bytes 524288 | tf_op jit(solution)/shard_map/all_to_all | solution.py:49
  56.9 3.8 collective-permute-start.1
  60.7 3.7 collective-permute-start.2
  145.1 7.0 %copy-start.38 = (f32[1024]{0:T(1024)S(1)}, f32[1024]{0:T(1024)}, u32[]{:S(2)}) copy-start(f32[1024]{0:T(1024)} %param.13) | copy-start | bytes 12292
  145.1 24.1 %copy-start.33 = (pred[2048]{0:T(1024)(128)(4,1)S(1)}, pred[2048]{0:T(1024)(128)(4,1)}, u32[]{:S(2)}) copy-start(pred[2048]{0:T(1024)(128)(4,1)} %copy-done.32) | copy-start | bytes 6148
  148.4 3.7 copy-start.11
  148.4 3.7 copy-start.13
  148.8 1.2 collective-permute-start.3
  150.1 17.6 %collective-permute-start.4 = (f32[2,32,16]{1,2,0:T(8,128)S(1)}, f32[2,32,16]{1,2,0:T(8,128)S(1)}, u32[]{:S(2)}, u32[]{:S(2)}) collective-permute-start(f32[2,32,16]{1,2,0:T(8,128)S(1)} %add.176), channel_id=1, source_target_pairs={{0,8},{4,12},{8,0},{12,4},{16,24},{20,28},{24,16},{28,20},{1,9},{5... | collective-permute-start | bytes 12296 | tf_op jit(solution)/shard_map/ppermute | solution.py:20
  167.7 17.0 %collective-permute-start.5 = (f32[2,32,16]{1,2,0:T(8,128)S(1)}, f32[2,32,16]{1,2,0:T(8,128)S(1)}, u32[]{:S(2)}, u32[]{:S(2)}) collective-permute-start(f32[2,32,16]{1,2,0:T(8,128)S(1)} %add.177), channel_id=1, source_target_pairs={{0,16},{4,20},{8,24},{12,28},{16,0},{20,4},{24,8},{28,12},{1,17},{... | collective-permute-start | bytes 12296 | tf_op jit(solution)/shard_map/ppermute | solution.py:20
  181.1 10.3 %all-to-all-start.1 = ((f32[2,16,8,256]{3,1,0,2:T(8,128)}), f32[2,16,8,256]{3,1,0,2:T(8,128)S(1)}, u32[]{:S(2)}, u32[]{:S(2)}) async-start(f32[2,16,8,256]{3,1,0,2:T(8,128)} %copy.139), calls=%async_computation.1 | async-start | bytes 524288 | tf_op jit(solution)/shard_map/all_to_all | solution.py:49
  257.3 10.4 %copy-start.9 = (f32[1024,2,16]{2,1,0:T(2,128)S(1)}, f32[1024,2,16]{2,1,0:T(2,128)}, u32[]{:S(2)}) copy-start(f32[1024,2,16]{2,1,0:T(2,128)} %gather_fusion.15) | copy-start | bytes 393220
  259.4 9.3 %copy-start.7 = (f32[1024,2,16]{2,1,0:T(2,128)S(1)}, f32[1024,2,16]{2,1,0:T(2,128)}, u32[]{:S(2)}) copy-start(f32[1024,2,16]{2,1,0:T(2,128)} %gather_fusion.16) | copy-start | bytes 393220
  261.5 7.6 %copy-start.5 = (f32[1024,2,16]{2,1,0:T(2,128)S(1)}, f32[1024,2,16]{2,1,0:T(2,128)}, u32[]{:S(2)}) copy-start(f32[1024,2,16]{2,1,0:T(2,128)} %gather_fusion.17) | copy-start | bytes 393220
  269.2 20.2 %copy-start.34 = (pred[2048]{0:T(1024)(128)(4,1)S(1)}, pred[2048]{0:T(1024)(128)(4,1)}, u32[]{:S(2)}) copy-start(pred[2048]{0:T(1024)(128)(4,1)} %copy-done.32) | copy-start | bytes 6148
  271.4 1.7 copy-start.15
  271.4 1.7 copy-start.17
  271.9 1.2 collective-permute-start.6
  273.2 15.6 %collective-permute-start.7 = (f32[2,32,16]{1,2,0:T(8,128)S(1)}, f32[2,32,16]{1,2,0:T(8,128)S(1)}, u32[]{:S(2)}, u32[]{:S(2)}) collective-permute-start(f32[2,32,16]{1,2,0:T(8,128)S(1)} %add.188), channel_id=1, source_target_pairs={{0,8},{4,12},{8,0},{12,4},{16,24},{20,28},{24,16},{28,20},{1,9},{5... | collective-permute-start | bytes 12296 | tf_op jit(solution)/shard_map/ppermute | solution.py:20
  288.8 16.1 %collective-permute-start.8 = (f32[2,32,16]{1,2,0:T(8,128)S(1)}, f32[2,32,16]{1,2,0:T(8,128)S(1)}, u32[]{:S(2)}, u32[]{:S(2)}) collective-permute-start(f32[2,32,16]{1,2,0:T(8,128)S(1)} %add.189), channel_id=1, source_target_pairs={{0,16},{4,20},{8,24},{12,28},{16,0},{20,4},{24,8},{28,12},{1,17},{... | collective-permute-start | bytes 12296 | tf_op jit(solution)/shard_map/ppermute | solution.py:20
  301.3 10.6 %all-to-all-start.2 = ((f32[2,16,8,256]{3,1,0,2:T(8,128)}), f32[2,16,8,256]{3,1,0,2:T(8,128)S(1)}, u32[]{:S(2)}, u32[]{:S(2)}) async-start(f32[2,16,8,256]{3,1,0,2:T(8,128)} %copy.158), calls=%async_computation.2 | async-start | bytes 524288 | tf_op jit(solution)/shard_map/all_to_all | solution.py:49
  377.8 10.4 %copy-start.10 = (f32[1024,2,16]{2,1,0:T(2,128)S(1)}, f32[1024,2,16]{2,1,0:T(2,128)}, u32[]{:S(2)}) copy-start(f32[1024,2,16]{2,1,0:T(2,128)} %gather_fusion.24) | copy-start | bytes 393220
  379.9 9.3 %copy-start.8 = (f32[1024,2,16]{2,1,0:T(2,128)S(1)}, f32[1024,2,16]{2,1,0:T(2,128)}, u32[]{:S(2)}) copy-start(f32[1024,2,16]{2,1,0:T(2,128)} %gather_fusion.25) | copy-start | bytes 393220
  382.0 7.6 %copy-start.6 = (f32[1024,2,16]{2,1,0:T(2,128)S(1)}, f32[1024,2,16]{2,1,0:T(2,128)}, u32[]{:S(2)}) copy-start(f32[1024,2,16]{2,1,0:T(2,128)} %gather_fusion.26) | copy-start | bytes 393220
  389.6 20.3 %copy-start.35 = (pred[2048]{0:T(1024)(128)(4,1)S(1)}, pred[2048]{0:T(1024)(128)(4,1)}, u32[]{:S(2)}) copy-start(pred[2048]{0:T(1024)(128)(4,1)} %copy-done.32) | copy-start | bytes 6148
  391.9 1.7 copy-start.19
  391.9 1.7 copy-start.21
  392.4 1.2 collective-permute-start.9
  393.6 15.6 %collective-permute-start.10 = (f32[2,32,16]{1,2,0:T(8,128)S(1)}, f32[2,32,16]{1,2,0:T(8,128)S(1)}, u32[]{:S(2)}, u32[]{:S(2)}) collective-permute-start(f32[2,32,16]{1,2,0:T(8,128)S(1)} %add.200), channel_id=1, source_target_pairs={{0,8},{4,12},{8,0},{12,4},{16,24},{20,28},{24,16},{28,20},{1,9},{5... | collective-permute-start | bytes 12296 | tf_op jit(solution)/shard_map/ppermute | solution.py:20
  409.3 16.3 %collective-permute-start.11 = (f32[2,32,16]{1,2,0:T(8,128)S(1)}, f32[2,32,16]{1,2,0:T(8,128)S(1)}, u32[]{:S(2)}, u32[]{:S(2)}) collective-permute-start(f32[2,32,16]{1,2,0:T(8,128)S(1)} %add.201), channel_id=1, source_target_pairs={{0,16},{4,20},{8,24},{12,28},{16,0},{20,4},{24,8},{28,12},{1,17},{... | collective-permute-start | bytes 12296 | tf_op jit(solution)/shard_map/ppermute | solution.py:20
  421.8 30.9 %copy-start.31 = (s32[1024]{0:T(1024)S(1)}, s32[1024]{0:T(1024)}, u32[]{:S(2)}) copy-start(s32[1024]{0:T(1024)} %fusion.111) | copy-start | bytes 12292
  421.8 38.5 %copy-start.30 = (s32[1024]{0:T(1024)S(1)}, s32[1024]{0:T(1024)}, u32[]{:S(2)}) copy-start(s32[1024]{0:T(1024)} %fusion.112) | copy-start | bytes 12292
  421.8 10.7 %all-to-all-start.3 = ((f32[2,16,8,256]{3,1,0,2:T(8,128)}), f32[2,16,8,256]{3,1,0,2:T(8,128)S(1)}, u32[]{:S(2)}, u32[]{:S(2)}) async-start(f32[2,16,8,256]{3,1,0,2:T(8,128)} %copy.177), calls=%async_computation.3 | async-start | bytes 524288 | tf_op jit(solution)/shard_map/all_to_all | solution.py:49
  498.1 6.2 %copy-start.1 = (f32[1024,2,16]{2,1,0:T(2,128)S(1)}, f32[1024,2,16]{2,1,0:T(2,128)}, u32[]{:S(2)}) copy-start(f32[1024,2,16]{2,1,0:T(2,128)} %gather_fusion.31) | copy-start | bytes 393220
  498.1 7.3 %copy-start.2 = (f32[1024,2,16]{2,1,0:T(2,128)S(1)}, f32[1024,2,16]{2,1,0:T(2,128)}, u32[]{:S(2)}) copy-start(f32[1024,2,16]{2,1,0:T(2,128)} %gather_fusion.32) | copy-start | bytes 393220
  498.1 8.4 %copy-start.3 = (f32[1024,2,16]{2,1,0:T(2,128)S(1)}, f32[1024,2,16]{2,1,0:T(2,128)}, u32[]{:S(2)}) copy-start(f32[1024,2,16]{2,1,0:T(2,128)} %gather_fusion.33) | copy-start | bytes 393220
  504.4 5.1 copy-start.28
  504.4 5.1 %copy-start.29 = (f32[1,1024]{1,0:T(1,128)S(1)}, f32[1,1024]{1,0:T(1,128)}, u32[]{:S(2)}) copy-start(f32[1,1024]{1,0:T(1,128)} %get-tuple-element.32) | copy-start | bytes 12292
  505.4 3.6 copy-start.4
  506.5 3.0 copy-start.20
  506.5 3.0 copy-start.22
  506.5 3.0 copy-start.23
  506.5 3.0 copy-start.24
  506.5 3.0 copy-start.25
  506.5 3.0 copy-start.26
  506.5 3.0 copy-start.27
  506.5 4.5 copy-start.12
  506.5 4.5 copy-start.14
  506.6 4.5 copy-start.16
  506.6 4.5 copy-start.18
